TPU v7x, 32 devices: a whole 2x2x4 slice. The times are simulated.
32 devices in a mesh: img: 8 (over y, x, core), head: 4 (over z).
Axes of the slice: x: 2, y: 2, z: 4, core: 2. Of those that a mesh axis runs over, the one named last changes fastest.
Arguments:
- tokens: bfloat16 [40, 256, 768], P('img'), may hold values from -6 to 6
- mask_embed: float32 [768], replicated, may hold values from -6 to 6
- norm_gains: float32 [2, 768], replicated, may hold values from 0.1 to 1.9
- norm_shifts: float32 [2, 768], replicated, may hold values from -4 to 4
- qkv_weight: bfloat16 [3, 768, 768], P(None, None, 'head'), may hold values from -0.3125 to 0.3125
- qv_bias: float32 [2, 768], P(None, 'head'), may hold values from -4 to 4
- out_weight: bfloat16 [768, 768], P('head'), may hold values from -0.4375 to 0.4375
- output_biases: float32 [2, 768], replicated, may hold values from -4 to 4
- up_weight: bfloat16 [768, 3072], P(None, 'head'), may hold values from -0.21875 to 0.21875
- up_bias: float32 [3072], P('head'), may hold values from -4 to 4
- down_weight: bfloat16 [3072, 768], P('head'), may hold values from -0.109375 to 0.109375
- counts: int32 [40], P('img'), may hold values from 1 to 256, as said below
- token_ranks: int32 [40, 256], P('img'), may hold values from 0 to 255, each once within a row
- cotangent: bfloat16 [40, 256, 768], P('img'), may hold values from -6 to 6
Outputs:
- out: bfloat16 [40, 256, 768], P('img')
- tokens_grad: float32 [40, 256, 768], P('img')
- mask_embed_grad: float32 [768], replicated
- norm_gains_grad: float32 [2, 768], replicated
- norm_shifts_grad: float32 [2, 768], replicated
- qkv_weight_grad: float32 [3, 768, 768], P(None, None, 'head')
- qv_bias_grad: float32 [2, 768], P(None, 'head')
- out_weight_grad: float32 [768, 768], P('head')
- output_biases_grad: float32 [2, 768], replicated
- up_weight_grad: float32 [768, 3072], P(None, 'head')
- up_bias_grad: float32 [3072], P('head')
- down_weight_grad: float32 [3072, 768], P('head')
Inputs may be any that keep to these rules, and one draw needn't show every extreme that they name: `counts`: each image's count follows the cosine masking plan over 256 tokens. `token_ranks`: each image's row is a permutation of 0 to 255.
All inputs are finite; a program needn't handle non-finite values.
Results may differ from a plain program's by a relative error of at most 0.012.
The roundings to bfloat16 on the way count: a program that leaves them out, or rounds other values in their place, can miss the bound.
Values sent between devices are 32-bit elements; how exact they have to be, the bound alone decides.
No kernel may reach another device: no remote copies, remote signals or barrier semaphores. Data moves between devices by JAX's collectives and lax.ppermute only.
A program may use at most 128 MiB of HBM per device.

v0:
```python
from functools import partial
import jax
import jax.numpy as jnp
from jax import lax
from jax.sharding import PartitionSpec as P

HEAD_DIM = 48
norm_eps = 1e-06


def contract_rows(left, right):
    return lax.dot_general(
        left, right, (((0,), (0,)), ((), ())), preferred_element_type=jnp.float32
    )


def times_transposed(left, right):
    return lax.dot_general(
        left, right, (((1,), (1,)), ((), ())), preferred_element_type=jnp.float32
    )


def normalize(values, scaling, offset):
    center = values - jnp.mean(values, axis=-1, keepdims=True)
    inverse = lax.rsqrt(jnp.mean(center * center, axis=-1, keepdims=True) + norm_eps)
    normal = center * inverse
    return (normal * scaling + offset, normal, inverse)


def normalize_back(upstream, normal, inverse, scaling):
    scaled = upstream * scaling
    inner = (
        scaled
        - jnp.mean(scaled, axis=-1, keepdims=True)
        - normal * jnp.mean(scaled * normal, axis=-1, keepdims=True)
    )
    return (inverse * inner, jnp.sum(upstream * normal, axis=0), jnp.sum(upstream, axis=0))


def forward(start, params, images, seq_len):
    (
        norm_gains,
        norm_shifts,
        qkv_weight,
        qv_bias,
        out_weight,
        output_biases,
        up_weight,
        up_bias,
        down_weight,
    ) = params
    local_width = qkv_weight.shape[2]
    head_shape = (images, seq_len, local_width // HEAD_DIM, HEAD_DIM)
    score_scale = HEAD_DIM ** (-0.5)
    attn_normed, attn_normal, attn_inverse = normalize(start, norm_gains[0], norm_shifts[0])
    attn_normed = attn_normed.astype(jnp.bfloat16)
    bias_rows = jnp.stack([qv_bias[0], jnp.zeros_like(qv_bias[0]), qv_bias[1]])
    projected = jnp.einsum(
        "td,ndc->ntc", attn_normed, qkv_weight, preferred_element_type=jnp.float32
    )
    projected = (projected + bias_rows[:, None, :]).astype(jnp.bfloat16)
    scores = (
        jnp.einsum(
            "bqhd,bkhd->bhqk",
            projected[0].reshape(head_shape),
            projected[1].reshape(head_shape),
            preferred_element_type=jnp.float32,
        )
        * score_scale
    )
    row_max = jnp.max(scores, axis=-1, keepdims=True)
    exponent = jnp.exp(scores - row_max)
    row_total = jnp.sum(exponent, axis=-1, keepdims=True)
    attn_probs = (exponent / row_total).astype(jnp.bfloat16)
    log_total = row_max + jnp.log(row_total)
    mixed = jnp.einsum(
        "bhqk,bkhd->bqhd",
        attn_probs,
        projected[2].reshape(head_shape),
        preferred_element_type=jnp.float32,
    )
    mixed = mixed.reshape(start.shape[0], local_width).astype(jnp.bfloat16)
    attended = lax.psum(jnp.dot(mixed, out_weight, preferred_element_type=jnp.float32), "head")
    after_attn = start + attended + output_biases[0]
    mlp_normed, mlp_normal, mlp_inverse = normalize(after_attn, norm_gains[1], norm_shifts[1])
    mlp_normed = mlp_normed.astype(jnp.bfloat16)
    pre_act = jnp.dot(mlp_normed, up_weight, preferred_element_type=jnp.float32) + up_bias
    activated = jax.nn.gelu(pre_act, approximate=True).astype(jnp.bfloat16)
    branch = lax.psum(jnp.dot(activated, down_weight, preferred_element_type=jnp.float32), "head")
    after_mlp = after_attn + branch + output_biases[1]
    saved = (
        attn_normal,
        attn_inverse,
        attn_normed,
        projected,
        log_total,
        mixed,
        mlp_normal,
        mlp_inverse,
        mlp_normed,
        pre_act,
        activated,
    )
    return (after_mlp, saved)


def per_device(
    tokens,
    mask_embed,
    norm_gains,
    norm_shifts,
    qkv_weight,
    qv_bias,
    out_weight,
    output_biases,
    up_weight,
    up_bias,
    down_weight,
    counts,
    token_ranks,
    cotangent,
):
    images, seq_len, model_width = tokens.shape
    row_count = images * seq_len
    local_width = qkv_weight.shape[2]
    head_shape = (images, seq_len, local_width // HEAD_DIM, HEAD_DIM)
    score_scale = HEAD_DIM ** (-0.5)
    local_count = jnp.sum(counts.astype(jnp.float32))
    masked_sum = lax.psum(local_count, "img")
    is_masked = (token_ranks < counts[:, None]).reshape(row_count, 1)
    mask_col = is_masked.astype(jnp.float32)
    start = jnp.where(
        is_masked, mask_embed[None, :], tokens.reshape(row_count, model_width).astype(jnp.float32)
    )
    params = (
        norm_gains,
        norm_shifts,
        qkv_weight,
        qv_bias,
        out_weight,
        output_biases,
        up_weight,
        up_bias,
        down_weight,
    )
    result, saved = forward(start, params, images, seq_len)
    again = lax.optimization_barrier((start, result))[0]
    unused, saved = forward(again, params, images, seq_len)
    (
        attn_normal,
        attn_inverse,
        attn_normed,
        projected,
        log_total,
        mixed,
        mlp_normal,
        mlp_inverse,
        mlp_normed,
        pre_act,
        activated,
    ) = saved
    signal = cotangent.reshape(row_count, model_width).astype(jnp.float32) * mask_col
    signal_low = signal.astype(jnp.bfloat16)
    down_bias_raw = jnp.sum(signal, axis=0)
    down_weight_raw = contract_rows(activated, signal_low)
    grad_act = times_transposed(signal_low, down_weight)
    unused_value, gelu_pull = jax.vjp(partial(jax.nn.gelu, approximate=True), pre_act)
    grad_pre = gelu_pull(grad_act)[0].astype(jnp.bfloat16)
    up_bias_raw = jnp.sum(grad_pre.astype(jnp.float32), axis=0)
    up_weight_raw = contract_rows(mlp_normed, grad_pre)
    grad_mlp_normed = lax.psum(times_transposed(grad_pre, up_weight), "head")
    grad_after, mlp_gain_raw, mlp_shift_raw = normalize_back(
        grad_mlp_normed, mlp_normal, mlp_inverse, norm_gains[1]
    )
    upper = signal + grad_after
    upper_low = upper.astype(jnp.bfloat16)
    out_bias_raw = jnp.sum(upper, axis=0)
    out_weight_raw = contract_rows(mixed, upper_low)
    grad_mixed = times_transposed(upper_low, out_weight).astype(jnp.bfloat16).reshape(head_shape)
    queries = projected[0].reshape(head_shape)
    keys_local = projected[1].reshape(head_shape)
    values_local = projected[2].reshape(head_shape)
    scores = (
        jnp.einsum("bqhd,bkhd->bhqk", queries, keys_local, preferred_element_type=jnp.float32)
        * score_scale
    )
    probs = jnp.exp(scores - log_total)
    probs_low = probs.astype(jnp.bfloat16)
    grad_probs = jnp.einsum(
        "bqhd,bkhd->bhqk", grad_mixed, values_local, preferred_element_type=jnp.float32
    )
    grad_values = jnp.einsum(
        "bhqk,bqhd->bkhd", probs_low, grad_mixed, preferred_element_type=jnp.float32
    )
    inner_sum = jnp.sum(probs * grad_probs, axis=-1, keepdims=True)
    grad_scores = (probs * (grad_probs - inner_sum) * score_scale).astype(jnp.bfloat16)
    grad_queries = jnp.einsum(
        "bhqk,bkhd->bqhd", grad_scores, keys_local, preferred_element_type=jnp.float32
    )
    grad_keys = jnp.einsum(
        "bhqk,bqhd->bkhd", grad_scores, queries, preferred_element_type=jnp.float32
    )
    grad_project = (
        jnp.stack([grad_queries, grad_keys, grad_values])
        .reshape(3, row_count, local_width)
        .astype(jnp.bfloat16)
    )
    qkv_weight_raw = jnp.einsum(
        "td,ntc->ndc", attn_normed, grad_project, preferred_element_type=jnp.float32
    )
    column_sums = jnp.sum(grad_project.astype(jnp.float32), axis=1)
    qv_bias_raw = jnp.stack([column_sums[0], column_sums[2]])
    grad_attn_normed = lax.psum(
        jnp.einsum("ntc,ndc->td", grad_project, qkv_weight, preferred_element_type=jnp.float32),
        "head",
    )
    grad_start, attn_gain_raw, attn_shift_raw = normalize_back(
        grad_attn_normed, attn_normal, attn_inverse, norm_gains[0]
    )
    lower = upper + grad_start
    mask_embed_raw = jnp.sum(lower * mask_col, axis=0)
    tokens_raw = lower * (1.0 - mask_col)
    gains_raw = jnp.stack([attn_gain_raw, mlp_gain_raw])
    shifts_raw = jnp.stack([attn_shift_raw, mlp_shift_raw])
    biases_raw = jnp.stack([out_bias_raw, down_bias_raw])
    summed = lax.psum(
        (
            mask_embed_raw,
            gains_raw,
            shifts_raw,
            qkv_weight_raw,
            qv_bias_raw,
            out_weight_raw,
            biases_raw,
            up_weight_raw,
            up_bias_raw,
            down_weight_raw,
        ),
        "img",
    )
    loss_scale = lax.axis_size("img") * row_count / masked_sum
    out = result.astype(jnp.bfloat16).reshape(images, seq_len, model_width)
    tokens_grad = (tokens_raw * loss_scale).reshape(images, seq_len, model_width)
    return (
        out,
        tokens_grad,
        summed[0] * loss_scale,
        summed[1] * loss_scale,
        summed[2] * loss_scale,
        summed[3] * loss_scale,
        summed[4] * loss_scale,
        summed[5] * loss_scale,
        summed[6] * loss_scale,
        summed[7] * loss_scale,
        summed[8] * loss_scale,
        summed[9] * loss_scale,
    )


def solution(mesh):
    return jax.shard_map(
        per_device,
        mesh=mesh,
        in_specs=(
            P("img", None, None),
            P(),
            P(),
            P(),
            P(None, None, "head"),
            P(None, "head"),
            P("head", None),
            P(),
            P(None, "head"),
            P("head"),
            P("head", None),
            P("img"),
            P("img", None),
            P("img", None, None),
        ),
        out_specs=(
            P("img", None, None),
            P("img", None, None),
            P(),
            P(),
            P(),
            P(None, None, "head"),
            P(None, "head"),
            P("head", None),
            P(),
            P(None, "head"),
            P("head"),
            P("head", None),
        ),
        check_vma=False,
    )
```

profile of v0, /device:TPU:0, one launch (start us, length us, event | category | flops | bytes accessed | tf_op | source)
XLA Modules:
  0.0 1022.0 jit_solution(18225187835026592122)
XLA Ops:
  23.9 5.7 fusion.141
  36.3 149.1 %all-reduce.9.cloned.1.call-done = f32[1280,768]{1,0:T(8,128)} async-done(((f32[1280,768]{1,0:T(8,128)}), f32[1280,768]{1,0:T(8,128)}) %all-reduce.9.cloned.1.call-update) | async-done | bytes 3932176 | tf_op jit(solution)/shard_map/psum | solution.py:83
  191.1 7.2 fusion.89
  198.3 145.6 %all-reduce.11.cloned.1.call-done = f32[1280,768]{1,0:T(8,128)} async-done(((f32[1280,768]{1,0:T(8,128)}), f32[1280,768]{1,0:T(8,128)}) %all-reduce.11.cloned.1.call-update) | async-done | bytes 3932176 | tf_op jit(solution)/shard_map/psum | solution.py:89
  343.9 5.1 add_add_fusion.1
  373.4 3.7 fusion.153
  377.1 140.0 %all-reduce.13.cloned.1.call-done = f32[1280,768]{1,0:T(8,128)} async-done(((f32[1280,768]{1,0:T(8,128)}), f32[1280,768]{1,0:T(8,128)}) %all-reduce.13.cloned.1.call-update) | async-done | bytes 3932176 | tf_op jit(solution)/shard_map/psum | solution.py:83
  517.1 3.8 fusion.135
  524.5 6.0 convert_reduce_fusion
  531.7 3.7 fusion.154
  535.8 145.2 %all-reduce.15.cloned.1.call-done = f32[1280,768]{1,0:T(8,128)} async-done(((f32[1280,768]{1,0:T(8,128)}), f32[1280,768]{1,0:T(8,128)}) %all-reduce.15.cloned.1.call-update) | async-done | bytes 3932176 | tf_op jit(solution)/shard_map/psum | solution.py:171
  681.0 4.7 multiply_reduce_fusion.4
  693.4 4.4 fusion.94
  697.7 4.3 fusion.76
  702.1 10.6 %fusion.82 = bf16[5,256,4,48]{1,3,2,0:T(8,128)(2,1)} fusion(f32[5,4,256,256]{2,3,1,0:T(8,128)} %fusion.94, f32[5,4,256,256]{2,3,1,0:T(8,128)} %copy-done.10, f32[5,4,256]{2,1,0:T(4,128)S(1)} %log_add_fusion, bf16[5,256,4,48]{1,0,3,2:T(8,128)(2,1)} %copy-done.23), kind=kOutput, calls=%fused_computation.104 | convolution fusion | flops 137876736 | bytes 11489280 | tf_op jit(solution)/shard_map/bhqk,bkhd->bqhd/dot_general | solution.py:197
  712.7 9.4 fusion.79
  734.4 4.8 convolution_bitcast_fusion
  739.3 6.4 fusion.131
  745.8 3.5 fusion.58
  757.0 127.9 %all-reduce.17.cloned.1.call-done = f32[1280,768]{1,0:T(8,128)} async-done(((f32[1280,768]{1,0:T(8,128)}), f32[1280,768]{1,0:T(8,128)}) %all-reduce.17.cloned.1.call-update) | async-done | bytes 3932176 | tf_op jit(solution)/shard_map/psum | solution.py:213
  884.9 5.2 multiply_reduce_fusion.5
  890.5 4.7 multiply_reduce_fusion.6
  895.2 26.4 %all-reduce = (f32[]{:T(128)}, f32[768]{0:T(1024)S(1)}, f32[2,768]{1,0:T(2,128)S(1)}, f32[2,768]{1,0:T(2,128)S(1)}, f32[2,192]{1,0:T(2,128)S(1)}, /*index=5*/f32[2,768]{1,0:T(2,128)S(1)}, f32[768]{0:T(1024)S(1)}) all-reduce(f32[]{:T(128)} %convert_reduce_fusion.2, ...), channel_id=1, replica_groups=mesh['img'=8,'head'=4] {'img'}, use_global_device_ids=true, to_apply=%region_23.24 | all-reduce | flops 6529 | bytes 52232 | tf_op jit(solution)/shard_map/psum | solution.py:129
  922.3 79.6 %all-reduce.19.cloned.1.call-done = (f32[3,768,192]{1,2,0:T(8,128)}, f32[192,768]{1,0:T(8,128)}, f32[768,768]{1,0:T(8,128)}, f32[768,768]{1,0:T(8,128)}) async-done(((f32[3,768,192]{1,2,0:T(8,128)}, f32[192,768]{1,0:T(8,128)}, f32[768,768]{1,0:T(8,128)}, f32[768,768]{1,0:T(8,128)}), (f32[3,768,192]{1,2,0:T(8,128)}, f32[192,768]{1,0:T(8,128)}, f32[768,768]{1,0:T(8,128)}, ...) | async-done | bytes 7077904 | tf_op jit(solution)/shard_map/psum | solution.py:226
  (197 shorter events, 99.3 us)
Async XLA Ops:
  7.2 183.9 %copy-start = (bf16[768,768]{1,0:T(8,128)(2,1)S(1)}, bf16[768,768]{1,0:T(8,128)(2,1)}, u32[]{:S(2)}) copy-start(bf16[768,768]{1,0:T(8,128)(2,1)} %param.22) | copy-start | bytes 3538948
  7.2 5.5 copy-start.31
  7.2 5.5 copy-start.12
  7.2 5.5 copy-start.35
  7.2 178.2 %all-reduce.9.cloned.1.call-start = ((), (), s32[]{:S(2)}) async-start(), calls=%async_computation | async-start | bytes 7864320 | tf_op jit(solution)/shard_map/psum | solution.py:83
  29.6 3.8 copy-start.18
  36.1 307.8 %all-reduce.11.cloned.1.call-start = ((), (), s32[]{:S(2)}) async-start(), calls=%async_computation.1 | async-start | bytes 7864320 | tf_op jit(solution)/shard_map/psum | solution.py:89
  198.3 318.8 %all-reduce.13.cloned.1.call-start = ((), (), s32[]{:S(2)}) async-start(), calls=%async_computation.2 | async-start | bytes 7864320 | tf_op jit(solution)/shard_map/psum | solution.py:83
  358.7 7.6 copy-start.22
  360.6 5.7 copy-start.23
  371.4 309.6 %all-reduce.15.cloned.1.call-start = ((), (), s32[]{:S(2)}) async-start(), calls=%async_computation.3 | async-start | bytes 7864320 | tf_op jit(solution)/shard_map/psum | solution.py:171
  520.9 9.5 copy-start.8
  520.9 3.5 copy-start.42
  535.4 349.5 %all-reduce.17.cloned.1.call-start = ((), (), s32[]{:S(2)}) async-start(), calls=%async_computation.4 | async-start | bytes 7864320 | tf_op jit(solution)/shard_map/psum | solution.py:213
  681.0 4.7 copy-start.9
  681.0 5.6 copy-start.15
  702.1 10.6 %copy-start.24 = (bf16[5,256,4,48]{1,0,3,2:T(8,128)(2,1)S(1)}, bf16[5,256,4,48]{1,0,3,2:T(8,128)(2,1)}, u32[]{:S(2)}) copy-start(bf16[5,256,4,48]{1,0,3,2:T(8,128)(2,1)} %reshape_squeeze.25) | copy-start | bytes 1474564
  739.3 262.6 %all-reduce.19.cloned.1.call-start = ((), (), s32[]{:S(2)}) async-start(), calls=%async_computation.5 | async-start | bytes 14155776 | tf_op jit(solution)/shard_map/psum | solution.py:226
  739.3 6.5 copy-start.28
  739.3 6.5 copy-start.43
  884.9 5.3 copy-start.4
  884.9 5.6 copy-start.7
  1001.9 4.9 copy-start.30
  1005.2 7.3 copy-start.14
  (27 other events, 57.9 us)
Sparse Core Ops, SparseCore 0:
  36.2 149.2 all-reduce.8
  198.4 145.4 all-reduce.10
  371.6 145.4 all-reduce.12
  535.5 145.4 all-reduce.14
  739.4 145.4 all-reduce.16
  889.6 112.2 all-reduce.18
where the time goes:
time: 1030 us; the launch traced here: 1020 us
  waiting for transfers between devices  787 us (76%)
  matrix products  90.1 us (9%)
  other arithmetic  58.6 us (6%)
  local copies, waits for them, and re-layouts  42.6 us (4%)
  blocking collectives  26.4 us (3%)
  between operations  15.8 us (2%)
    psum x2, waiting for transfers between devices, forward(): lax.psum(jnp.dot(mixed, out_weight, preferred_element_type=jnp.float32),...  289 us
    psum x1, waiting for transfers between devices, forward(): lax.psum(jnp.dot(activated, down_weight, preferred_element_type=jnp.float...  146 us
    psum x1, waiting for transfers between devices, per_device(): grad_mlp_normed = lax.psum(times_transposed(grad_pre, up_weight), 'head')  145 us
    psum x1, waiting for transfers between devices, per_device(): lax.psum(jnp.einsum('ntc,ndc->td', grad_project, qkv_weight, preferred_el...  128 us
    psum x1, waiting for transfers between devices, per_device(): lax.psum((mask_embed_raw, gains_raw, shifts_raw, qkv_weight_raw, qv_bias_...  79.6 us
    psum x1, blocking collectives, per_device(): masked_sum = lax.psum(local_count, 'img')  26.4 us
  transfers between devices with their start and end apart: 6, of which 6 were waited for; matrix products, arithmetic and copies ran while one was open for 3% of the time, Pallas kernels for 0%

commit v1 on v0

--- a/solution.py
+++ b/solution.py
@@ -86,7 +86,10 @@
     mlp_normed = mlp_normed.astype(jnp.bfloat16)
     pre_act = jnp.dot(mlp_normed, up_weight, preferred_element_type=jnp.float32) + up_bias
     activated = jax.nn.gelu(pre_act, approximate=True).astype(jnp.bfloat16)
-    branch = lax.psum(jnp.dot(activated, down_weight, preferred_element_type=jnp.float32), "head")
+    branch = jnp.sum(
+        lax.all_gather(jnp.dot(activated, down_weight, preferred_element_type=jnp.float32), "head"),
+        axis=0,
+    )
     after_mlp = after_attn + branch + output_biases[1]
     saved = (
         attn_normal,

time: 1030 us -> 1170 us (1.14)
  waiting for transfers between devices: 787 us -> 897 us
    all_gather x0 -> x1, waiting for transfers between devices: none -> 269 us  [forward(): lax.all_gather(jnp.dot(activated, down_weight, preferred_element_type=jnp...]
    psum x1 -> x0, waiting for transfers between devices: 146 us -> none  [forward(): lax.psum(jnp.dot(activated, down_weight, preferred_element_type=jnp.float...]
    psum x2, waiting for transfers between devices: 289 us -> 276 us  [forward(): lax.psum(jnp.dot(mixed, out_weight, preferred_element_type=jnp.float32),...]
    psum x1, starting transfers between devices: 0.25 us -> 12.2 us  [per_device(): grad_mlp_normed = lax.psum(times_transposed(grad_pre, up_weight), 'head')]
where the time goes in v1:
time: 1170 us; the launch traced here: 1160 us
  waiting for transfers between devices  897 us (77%)
  matrix products  92.3 us (8%)
  other arithmetic  68 us (6%)
  local copies, waits for them, and re-layouts  50.5 us (4%)
  blocking collectives  26.4 us (2%)
  between operations  16 us (1%)
  starting transfers between devices  12.7 us (1%)
    psum x2, waiting for transfers between devices, forward(): lax.psum(jnp.dot(mixed, out_weight, preferred_element_type=jnp.float32),...  276 us
    all_gather x1, waiting for transfers between devices, forward(): lax.all_gather(jnp.dot(activated, down_weight, preferred_element_type=jnp...  269 us
    psum x1, waiting for transfers between devices, per_device(): grad_mlp_normed = lax.psum(times_transposed(grad_pre, up_weight), 'head')  146 us
    psum x1, waiting for transfers between devices, per_device(): lax.psum(jnp.einsum('ntc,ndc->td', grad_project, qkv_weight, preferred_el...  127 us
    psum x1, waiting for transfers between devices, per_device(): lax.psum((mask_embed_raw, gains_raw, shifts_raw, qkv_weight_raw, qv_bias_...  79.6 us
    psum x1, blocking collectives, per_device(): masked_sum = lax.psum(local_count, 'img')  26.4 us
  transfers between devices with their start and end apart: 6, of which 6 were waited for; matrix products, arithmetic and copies ran while one was open for 3% of the time, Pallas kernels for 0%

profile of v1, /device:TPU:0, one launch (start us, length us, event | category | flops | bytes accessed | tf_op | source)
XLA Modules:
  0.0 1162.8 jit_solution(15082226573791682832)
XLA Ops:
  24.5 5.7 fusion.141
  37.0 149.0 %all-reduce.8.cloned.1.call-done = f32[1280,768]{1,0:T(8,128)} async-done(((f32[1280,768]{1,0:T(8,128)}), f32[1280,768]{1,0:T(8,128)}) %all-reduce.8.cloned.1.call-update) | async-done | bytes 3932176 | tf_op jit(solution)/shard_map/psum | solution.py:83
  191.7 7.2 fusion.89
  198.9 268.7 %all-gather.3.cloned.1.call-done = f32[5120,768]{1,0:T(8,128)} async-done(((f32[1280,768]{1,0:T(8,128)}), f32[5120,768]{1,0:T(8,128)}) %all-gather.3.cloned.1.call-update) | async-done | bytes 15728656 | tf_op jit(solution)/shard_map/all_gather | solution.py:90
  467.6 8.9 reduce_sum.239
  476.6 5.1 add_add_fusion.1
  504.1 12.2 %all-reduce.12.cloned.1.call-start = ((), (), s32[]{:S(2)}) async-start(), calls=%async_computation.2 | async-start | bytes 7864320 | tf_op jit(solution)/shard_map/psum | solution.py:174
  518.0 3.7 fusion.153
  521.7 127.2 %all-reduce.10.cloned.1.call-done = f32[1280,768]{1,0:T(8,128)} async-done(((f32[1280,768]{1,0:T(8,128)}), f32[1280,768]{1,0:T(8,128)}) %all-reduce.10.cloned.1.call-update) | async-done | bytes 3932176 | tf_op jit(solution)/shard_map/psum | solution.py:83
  648.9 3.8 fusion.135
  656.3 6.5 convert_reduce_fusion
  667.8 145.6 %all-reduce.12.cloned.1.call-done = f32[1280,768]{1,0:T(8,128)} async-done(((f32[1280,768]{1,0:T(8,128)}), f32[1280,768]{1,0:T(8,128)}) %all-reduce.12.cloned.1.call-update) | async-done | bytes 3932176 | tf_op jit(solution)/shard_map/psum | solution.py:174
  813.4 4.9 multiply_reduce_fusion.4
  826.5 4.8 fusion.94
  831.2 4.4 fusion.76
  835.6 10.7 fusion.82
  846.3 10.7 fusion.79
  875.1 4.8 convolution_bitcast_fusion
  880.6 6.4 fusion.131
  898.8 126.8 %all-reduce.14.cloned.1.call-done = f32[1280,768]{1,0:T(8,128)} async-done(((f32[1280,768]{1,0:T(8,128)}), f32[1280,768]{1,0:T(8,128)}) %all-reduce.14.cloned.1.call-update) | async-done | bytes 3932176 | tf_op jit(solution)/shard_map/psum | solution.py:216
  1025.6 4.9 multiply_reduce_fusion.5
  1031.2 4.7 multiply_reduce_fusion.6
  1035.9 26.4 %all-reduce = (f32[]{:T(128)}, f32[768]{0:T(1024)S(1)}, f32[2,768]{1,0:T(2,128)S(1)}, f32[2,768]{1,0:T(2,128)S(1)}, f32[2,192]{1,0:T(2,128)S(1)}, /*index=5*/f32[2,768]{1,0:T(2,128)S(1)}, f32[768]{0:T(1024)S(1)}) all-reduce(f32[]{:T(128)} %convert_reduce_fusion.2, ...), channel_id=1, replica_groups=mesh['img'=8,'head'=4] {'img'}, use_global_device_ids=true, to_apply=%region_23.24 | all-reduce | flops 6529 | bytes 52232 | tf_op jit(solution)/shard_map/psum | solution.py:132
  1063.0 79.6 %all-reduce.16.cloned.1.call-done = (f32[3,768,192]{1,2,0:T(8,128)}, f32[192,768]{1,0:T(8,128)}, f32[768,768]{1,0:T(8,128)}, f32[768,768]{1,0:T(8,128)}) async-done(((f32[3,768,192]{1,2,0:T(8,128)}, f32[192,768]{1,0:T(8,128)}, f32[768,768]{1,0:T(8,128)}, f32[768,768]{1,0:T(8,128)}), (f32[3,768,192]{1,2,0:T(8,128)}, f32[192,768]{1,0:T(8,128)}, f32[768,768]{1,0:T(8,128)}, ...) | async-done | bytes 7077904 | tf_op jit(solution)/shard_map/psum | solution.py:229
  (204 shorter events, 114.3 us)
Async XLA Ops:
  7.2 184.5 %copy-start = (bf16[768,768]{1,0:T(8,128)(2,1)S(1)}, bf16[768,768]{1,0:T(8,128)(2,1)}, u32[]{:S(2)}) copy-start(bf16[768,768]{1,0:T(8,128)(2,1)} %param.22) | copy-start | bytes 3538948
  7.2 6.1 copy-start.30
  7.2 6.1 copy-start.11
  7.2 6.1 copy-start.38
  7.2 178.8 %all-reduce.8.cloned.1.call-start = ((), (), s32[]{:S(2)}) async-start(), calls=%async_computation | async-start | bytes 7864320 | tf_op jit(solution)/shard_map/psum | solution.py:83
  13.9 639.5 %copy-start.35 = (f32[768]{0:T(1024)}, f32[768]{0:T(1024)S(1)}, u32[]{:S(2)}) copy-start(f32[768]{0:T(1024)S(1)} %get-tuple-element.26) | copy-start | bytes 9220
  36.7 431.0 %all-gather.3.cloned.1.call-start = ((), (), s32[]{:S(2)}) async-start(), calls=%async_computation.4 | async-start | bytes 19660800 | tf_op jit(solution)/shard_map/all_gather | solution.py:90
  198.9 450.0 %all-reduce.10.cloned.1.call-start = ((), (), s32[]{:S(2)}) async-start(), calls=%async_computation.1 | async-start | bytes 7864320 | tf_op jit(solution)/shard_map/psum | solution.py:83
  491.3 7.6 copy-start.22
  493.2 5.7 copy-start.23
  501.4 14.9 %copy-start.12 = (bf16[5,256,768]{2,1,0:T(8,128)(2,1)S(1)}, bf16[5,256,768]{2,1,0:T(8,128)(2,1)}, u32[]{:S(2)}) copy-start(bf16[5,256,768]{2,1,0:T(8,128)(2,1)} %param.27) | copy-start | bytes 5898244
  504.1 309.3 %all-reduce.12.cloned.1.call-start = ((), (), s32[]{:S(2)}) async-start(), calls=%async_computation.2 | async-start | bytes 7864320 | tf_op jit(solution)/shard_map/psum | solution.py:174
  652.8 10.0 copy-start.7
  667.8 357.8 %all-reduce.14.cloned.1.call-start = ((), (), s32[]{:S(2)}) async-start(), calls=%async_computation.3 | async-start | bytes 7864320 | tf_op jit(solution)/shard_map/psum | solution.py:216
  813.4 5.0 copy-start.8
  813.4 5.6 copy-start.14
  826.5 4.8 copy-start.17
  880.0 262.6 %all-reduce.16.cloned.1.call-start = ((), (), s32[]{:S(2)}) async-start(), calls=%async_computation.5 | async-start | bytes 14155776 | tf_op jit(solution)/shard_map/psum | solution.py:229
  880.6 6.4 copy-start.27
  880.6 6.4 copy-start.46
  1025.6 5.0 copy-start.3
  1025.6 5.6 copy-start.6
  1142.6 4.9 copy-start.29
  1146.0 7.3 copy-start.13
  (30 other events, 66.7 us)
Sparse Core Ops, SparseCore 0:
  36.8 149.2 all-reduce.7
  199.0 268.5 all-gather.2
  504.2 144.6 all-reduce.9
  667.9 145.4 all-reduce.11
  880.1 145.4 all-reduce.13
  1030.3 112.2 all-reduce.15
